TPU v7x, 512 devices: a whole 4x4x16 slice. The times are simulated.
512 devices in a mesh: region: 64 (over z, x), split: 8 (over y, core).
Axes of the slice: x: 4, y: 4, z: 16, core: 2. Of those that a mesh axis runs over, the one named last changes fastest.
Arguments:
- vectors: float32 [294912, 256], P(('region', 'split'))
- hessian: bfloat16 [1536, 12, 192, 192], P(('region', 'split')), may hold values from -0.125 to 0.125
- block_cols: int32 [1536, 12], P(('region', 'split')), may hold values from 0 to 35, as said below
- live_blocks: int32 [1536], P(('region', 'split')), may hold values from 6 to 12, as said below
- halo_lists: int32 [64, 2, 6], P('region'), may hold values from 0 to 23, as said below
- bounds: float32 [2], replicated, as said below
Outputs:
- basis: float32 [294912, 256], P(('region', 'split'))
- projected: float32 [256, 256], replicated
Inputs may be any that keep to these rules, and one draw needn't show every extreme that they name: `block_cols`: in each row the entries are distinct and entry 0 is the row's own block within its region; values below 24 name blocks of the row's region, 24 + j the j-th block received from the lower region, 30 + j the j-th from the upper region. `live_blocks`: the first block row of every region has all 12 blocks intact. `halo_lists`: each list holds distinct block indices within the region. bounds[0] < 0 < bounds[1].
All inputs are finite; a program needn't handle non-finite values.
Results may differ from a plain program's by a relative error of at most 0.0005.
The roundings to bfloat16 on the way count: a program that leaves them out, or rounds other values in their place, can miss the bound.
Values may be sent and summed in bfloat16 or wider, within the bound.
A program may use at most 64 MiB of HBM per device.

v0:
```python
import jax
import jax.numpy as jnp
from jax import lax
from jax.sharding import PartitionSpec as P


def shifted(value, axis, steps):
    count = lax.axis_size(axis)
    pairs = [(source, (source + steps) % count) for source in range(count)]
    return lax.ppermute(value, axis, pairs)


def apply_blocks(operand, hessian, block_cols, live_blocks, halo_lists):
    row_blocks = hessian.shape[0]
    block_size = hessian.shape[2]
    mode_count = operand.shape[1]
    shard_blocks = operand.reshape(row_blocks, block_size, mode_count)
    region = lax.all_gather(shard_blocks, "split", axis=0, tiled=True)
    send_lower = region[halo_lists[0, 0]]
    send_upper = region[halo_lists[0, 1]]
    from_lower = shifted(send_upper, "region", 1)
    from_upper = shifted(send_lower, "region", -1)
    candidates = jnp.concatenate([region, from_lower, from_upper], 0)
    picked = candidates[block_cols]
    used_mask = lax.broadcasted_iota(jnp.int32, block_cols.shape, 1) < live_blocks[:, None]
    picked = jnp.where(used_mask[:, :, None, None], picked, jnp.zeros((), jnp.bfloat16))
    product = jnp.einsum("rkij,rkjm->rim", hessian, picked, preferred_element_type=jnp.float32)
    return product.reshape(row_blocks * block_size, mode_count)


def local(vectors, hessian, block_cols, live_blocks, halo_lists, bounds):
    centre = 0.5 * (bounds[0] + bounds[1])
    half_width = 0.5 * (bounds[1] - bounds[0])
    first = apply_blocks(vectors.astype(jnp.bfloat16), hessian, block_cols, live_blocks, halo_lists)
    filtered_one = (first - centre * vectors) / half_width
    second = apply_blocks(
        filtered_one.astype(jnp.bfloat16), hessian, block_cols, live_blocks, halo_lists
    )
    filtered_two = 2.0 * (second - centre * filtered_one) / half_width - vectors
    image = apply_blocks(
        filtered_two.astype(jnp.bfloat16), hessian, block_cols, live_blocks, halo_lists
    )
    total_rows = vectors.shape[0] * lax.axis_size("region") * lax.axis_size("split")
    contract = (((0,), (0,)), ((), ()))
    gram_part = lax.dot_general(
        filtered_two, filtered_two, contract, precision=lax.Precision.HIGHEST
    )
    cross_part = lax.dot_general(filtered_two, image, contract, precision=lax.Precision.HIGHEST)
    gram, cross = lax.psum((gram_part, cross_part), ("region", "split"))
    gram = gram / total_rows
    cross = cross / total_rows
    lower = jnp.linalg.cholesky(gram)
    basis = jax.scipy.linalg.solve_triangular(lower, filtered_two.T, lower=True).T
    partial_left = jax.scipy.linalg.solve_triangular(lower, cross, lower=True)
    projected = jax.scipy.linalg.solve_triangular(lower, partial_left.T, lower=True).T
    return (basis, projected)


def solution(mesh):
    placed = (
        P(("region", "split"), None),
        P(("region", "split"), None, None, None),
        P(("region", "split"), None),
        P(("region", "split")),
        P("region", None, None),
        P(),
    )
    return jax.shard_map(
        local,
        mesh=mesh,
        in_specs=placed,
        out_specs=(P(("region", "split"), None), P()),
        check_vma=False,
    )
```

profile of v0, /device:TPU:1, one launch (start us, length us, event | category | flops | bytes accessed | tf_op | source)
XLA Modules:
  0.0 814.2 jit_solution(8782221556383976657)
XLA Ops:
  10.1 39.6 %all-gather.4.cloned.1.call-done = bf16[24,192,256]{2,1,0:T(8,128)(2,1)} async-done(((bf16[3,192,256]{2,1,0:T(8,128)(2,1)}), bf16[24,192,256]{2,1,0:T(8,128)(2,1)}) %all-gather.4.cloned.1.call-update) | async-done | bytes 2359312 | tf_op jit(solution)/shard_map/all_gather | solution.py:18
  59.0 6.6 collective-permute-start.1
  69.7 4.6 collective-permute-done
  74.3 4.0 collective-permute-done.1
  78.3 3.4 pad_maximum_fusion
  81.7 4.8 gather_fusion.2
  90.6 34.4 %all-gather.6.cloned.1.call-done = bf16[24,192,256]{2,1,0:T(8,128)(2,1)} async-done(((bf16[3,192,256]{2,1,0:T(8,128)(2,1)}), bf16[24,192,256]{2,1,0:T(8,128)(2,1)}) %all-gather.6.cloned.1.call-update) | async-done | bytes 2359312 | tf_op jit(solution)/shard_map/all_gather | solution.py:18
  134.3 6.6 collective-permute-start.3
  141.0 8.7 %collective-permute-done.2 = bf16[6,192,256]{2,1,0:T(8,128)(2,1)} collective-permute-done((bf16[6,192,256]{2,1,0:T(8,128)(2,1)}, bf16[6,192,256]{2,1,0:T(8,128)(2,1)}, u32[]{:S(2)}, u32[]{:S(2)}) %collective-permute-start.2) | collective-permute-done | bytes 589856 | tf_op jit(solution)/shard_map/ppermute | solution.py:10
  149.7 4.0 collective-permute-done.3
  153.7 3.3 pad_maximum_fusion.1
  157.0 4.8 gather_fusion.5
  166.1 34.3 %all-gather.8.cloned.1.call-done = bf16[24,192,256]{2,1,0:T(8,128)(2,1)} async-done(((bf16[3,192,256]{2,1,0:T(8,128)(2,1)}), bf16[24,192,256]{2,1,0:T(8,128)(2,1)}) %all-gather.8.cloned.1.call-update) | async-done | bytes 2359312 | tf_op jit(solution)/shard_map/all_gather | solution.py:18
  209.8 6.6 collective-permute-start.5
  219.6 5.5 collective-permute-done.4
  225.1 4.0 collective-permute-done.5
  229.1 3.3 pad_maximum_fusion.2
  232.5 4.8 gather_fusion.8
  242.3 466.4 %all-reduce.4.cloned.1.call-done = (f32[256,256]{0,1:T(8,128)}, f32[256,256]{0,1:T(8,128)}) async-done(((f32[256,256]{0,1:T(8,128)}, f32[256,256]{0,1:T(8,128)}), (f32[256,256]{0,1:T(8,128)}, f32[256,256]{0,1:T(8,128)})) %all-reduce.4.cloned.1.call-update) | async-done | bytes 524304 | tf_op jit(solution)/shard_map/psum | solution.py:49
  714.8 13.2 %cholesky.50 = f32[128,128]{1,0:T(8,128)} custom-call(f32[128,128]{1,0:T(8,128)} %cholesky.118), custom_call_target="Cholesky" | custom-call | tf_op jit(solution)/shard_map/jit(cholesky)/cholesky | solution.py:52
  731.0 11.3 %custom-call.18 = f32[1,128,128]{1,2,0:T(8,128)} custom-call(f32[1,128,128]{2,1,0:T(8,128)} %get-tuple-element.48), custom_call_target="InvertDiagBlocksLowerTriangular" | custom-call | tf_op jit(solution)/shard_map/jit(cholesky)/cholesky | solution.py:52
  745.7 13.4 %cholesky.105 = f32[128,128]{1,0:T(8,128)} custom-call(f32[128,128]{1,0:T(8,128)} %convolution_subtract_fusion.3), custom_call_target="Cholesky" | custom-call | tf_op jit(solution)/shard_map/jit(cholesky)/cholesky | solution.py:52
  765.0 6.9 while.5
  771.8 21.1 %custom-call.19 = f32[2,128,128]{1,2,0:T(8,128)} custom-call(f32[2,128,128]{2,1,0:T(8,128)} %get-tuple-element.18), custom_call_target="InvertDiagBlocksLowerTriangular" | custom-call | tf_op jit(solution)/shard_map/jit(_solve_triangular)/triangular_solve | solution.py:53
  (85 shorter events, 87.2 us)
Async XLA Ops:
  7.2 79.4 %copy-start = (bf16[3,12,192,192]{3,2,1,0:T(8,128)(2,1)S(1)}, bf16[3,12,192,192]{3,2,1,0:T(8,128)(2,1)}, u32[]{:S(2)}) copy-start(bf16[3,12,192,192]{3,2,1,0:T(8,128)(2,1)} %param.9) | copy-start | bytes 7962628
  7.2 58.4 %copy-start.8 = (f32[2]{0:T(128)S(1)}, f32[2]{0:T(128)}, u32[]{:S(2)}) copy-start(f32[2]{0:T(128)} %param.13) | copy-start | bytes 28
  7.2 61.7 %copy-start.7 = (s32[3,12]{1,0:T(4,128)S(1)}, s32[3,12]{1,0:T(4,128)}, u32[]{:S(2)}) copy-start(s32[3,12]{1,0:T(4,128)} %param.10) | copy-start | bytes 436
  7.2 42.5 %all-gather.4.cloned.1.call-start = ((), (), s32[]{:S(2)}) async-start(), calls=%async_computation | async-start | bytes 2654208 | tf_op jit(solution)/shard_map/all_gather | solution.py:18
  9.2 115.8 %all-gather.6.cloned.1.call-start = ((), (), s32[]{:S(2)}) async-start(), calls=%async_computation.1 | async-start | bytes 2654208 | tf_op jit(solution)/shard_map/all_gather | solution.py:18
  52.8 21.5 %collective-permute-start = (bf16[6,192,256]{2,1,0:T(8,128)(2,1)}, bf16[6,192,256]{2,1,0:T(8,128)(2,1)}, u32[]{:S(2)}, u32[]{:S(2)}) collective-permute-start(bf16[6,192,256]{2,1,0:T(8,128)(2,1)} %gather_fusion), channel_id=1, source_target_pairs={{0,8},{8,16},{16,24},{24,32},{32,40},{40,48},{48,56},{56,64},{64,7... | collective-permute-start | bytes 1769480 | tf_op jit(solution)/shard_map/ppermute | solution.py:10
  59.0 19.3 %collective-permute-start.1 = (bf16[6,192,256]{2,1,0:T(8,128)(2,1)}, bf16[6,192,256]{2,1,0:T(8,128)(2,1)}, u32[]{:S(2)}, u32[]{:S(2)}) collective-permute-start(bf16[6,192,256]{2,1,0:T(8,128)(2,1)} %gather_fusion.1), channel_id=1, source_target_pairs={{0,504},{8,0},{16,8},{24,16},{32,24},{40,32},{48,40},{56,48},{64,5... | collective-permute-start | bytes 1769480 | tf_op jit(solution)/shard_map/ppermute | solution.py:10
  86.6 3.1 copy-start.2
  89.6 0.9 copy-start.4
  90.6 109.9 %all-gather.8.cloned.1.call-start = ((), (), s32[]{:S(2)}) async-start(), calls=%async_computation.2 | async-start | bytes 2654208 | tf_op jit(solution)/shard_map/all_gather | solution.py:18
  128.1 21.5 %collective-permute-start.2 = (bf16[6,192,256]{2,1,0:T(8,128)(2,1)}, bf16[6,192,256]{2,1,0:T(8,128)(2,1)}, u32[]{:S(2)}, u32[]{:S(2)}) collective-permute-start(bf16[6,192,256]{2,1,0:T(8,128)(2,1)} %gather_fusion.3), channel_id=1, source_target_pairs={{0,8},{8,16},{16,24},{24,32},{32,40},{40,48},{48,56},{56,64},{64,7... | collective-permute-start | bytes 1769480 | tf_op jit(solution)/shard_map/ppermute | solution.py:10
  134.3 19.3 %collective-permute-start.3 = (bf16[6,192,256]{2,1,0:T(8,128)(2,1)}, bf16[6,192,256]{2,1,0:T(8,128)(2,1)S(1)}, u32[]{:S(2)}, u32[]{:S(2)}) collective-permute-start(bf16[6,192,256]{2,1,0:T(8,128)(2,1)} %gather_fusion.4), channel_id=1, source_target_pairs={{0,504},{8,0},{16,8},{24,16},{32,24},{40,32},{48,40},{56,48},{64,5... | collective-permute-start | bytes 1769480 | tf_op jit(solution)/shard_map/ppermute | solution.py:10
  161.9 3.1 copy-start.3
  161.9 3.1 copy-start.5
  166.1 542.7 %all-reduce.4.cloned.1.call-start = ((), (), s32[]{:S(2)}) async-start(), calls=%async_computation.3 | async-start | bytes 1048576 | tf_op jit(solution)/shard_map/psum | solution.py:49
  203.6 21.5 %collective-permute-start.4 = (bf16[6,192,256]{2,1,0:T(8,128)(2,1)}, bf16[6,192,256]{2,1,0:T(8,128)(2,1)}, u32[]{:S(2)}, u32[]{:S(2)}) collective-permute-start(bf16[6,192,256]{2,1,0:T(8,128)(2,1)} %gather_fusion.6), channel_id=1, source_target_pairs={{0,8},{8,16},{16,24},{24,32},{32,40},{40,48},{48,56},{56,64},{64,7... | collective-permute-start | bytes 1769480 | tf_op jit(solution)/shard_map/ppermute | solution.py:10
  209.8 19.3 %collective-permute-start.5 = (bf16[6,192,256]{2,1,0:T(8,128)(2,1)}, bf16[6,192,256]{2,1,0:T(8,128)(2,1)S(1)}, u32[]{:S(2)}, u32[]{:S(2)}) collective-permute-start(bf16[6,192,256]{2,1,0:T(8,128)(2,1)} %gather_fusion.7), channel_id=1, source_target_pairs={{0,504},{8,0},{16,8},{24,16},{32,24},{40,32},{48,40},{56,48},{64,5... | collective-permute-start | bytes 1769480 | tf_op jit(solution)/shard_map/ppermute | solution.py:10
  237.3 3.0 copy-start.1
  713.5 0.7 copy-start.6
Sparse Core Ops, SparseCore 0:
  10.7 38.9 all-gather.3
  90.7 34.3 all-gather.5
  166.2 34.2 all-gather.7
  242.4 466.3 all-reduce.3
where the time goes:
time: 816 us; the launch traced here: 814 us
  waiting for transfers between devices  606 us (74%)
  other arithmetic  85.1 us (10%)
  local copies, waits for them, and re-layouts  47.2 us (6%)
  starting transfers between devices  29.3 us (4%)
  matrix products  29 us (4%)
  between operations  18 us (2%)
    psum x1, waiting for transfers between devices, local(): gram, cross = lax.psum((gram_part, cross_part), ('region', 'split'))  466 us
    all_gather x3, waiting for transfers between devices, apply_blocks(): region = lax.all_gather(shard_blocks, 'split', axis=0, tiled=True)  108 us
    another operation x7, other arithmetic, local(): lower = jnp.linalg.cholesky(gram)  42.1 us
    ppermute x6, waiting for transfers between devices, shifted(): return lax.ppermute(value, axis, pairs)  30.8 us
    ppermute x6, starting transfers between devices, shifted(): return lax.ppermute(value, axis, pairs)  29.1 us
    another operation x3, other arithmetic, local(): jax.scipy.linalg.solve_triangular(lower, filtered_two.T, lower=True)  22.8 us
  transfers between devices with their start and end apart: 10, of which 10 were waited for; matrix products, arithmetic and copies ran while one was open for 2% of the time, Pallas kernels for 0%

commit v1 on v0

--- a/solution.py
+++ b/solution.py
@@ -2,6 +2,7 @@
 import jax.numpy as jnp
 from jax import lax
 from jax.sharding import PartitionSpec as P
+from jax.lax import all_to_all, axis_size
 
 
 def shifted(value, axis, steps):
@@ -15,7 +16,9 @@
     block_size = hessian.shape[2]
     mode_count = operand.shape[1]
     shard_blocks = operand.reshape(row_blocks, block_size, mode_count)
-    region = lax.all_gather(shard_blocks, "split", axis=0, tiled=True)
+    passed = jnp.stack([shard_blocks for _ in range(axis_size("split"))])
+    h_now = all_to_all(passed, "split", 0, 0)
+    region = jnp.concatenate(h_now, 0)
     send_lower = region[halo_lists[0, 0]]
     send_upper = region[halo_lists[0, 1]]
     from_lower = shifted(send_upper, "region", 1)

time: 816 us -> 810 us (level)
  waiting for transfers between devices: 606 us -> 521 us
  blocking collectives: 0 us -> 68 us
  starting transfers between devices: 29.3 us -> 39.8 us
    all_gather x3 -> x0, waiting for transfers between devices: 108 us -> none  [apply_blocks(): region = lax.all_gather(shard_blocks, 'split', axis=0, tiled=True)]
    all_to_all x0 -> x2, blocking collectives: none -> 68 us  [apply_blocks(): h_now = all_to_all(passed, 'split', 0, 0)]
    all_to_all x0 -> x1, waiting for transfers between devices: none -> 29.1 us  [apply_blocks(): h_now = all_to_all(passed, 'split', 0, 0)]
    all_to_all x0 -> x1, starting transfers between devices: none -> 11.2 us  [apply_blocks(): h_now = all_to_all(passed, 'split', 0, 0)]
  transfers between devices with their start and end apart: 10 -> 8, of which waited for: 10 -> 8; matrix products, arithmetic and copies ran while one was open for 2% -> 1% of each run, Pallas kernels for 0% -> 0%
where the time goes in v1:
time: 810 us; the launch traced here: 808 us
  waiting for transfers between devices  521 us (64%)
  other arithmetic  82.5 us (10%)
  blocking collectives  68 us (8%)
  local copies, waits for them, and re-layouts  49.4 us (6%)
  starting transfers between devices  39.8 us (5%)
  matrix products  29.1 us (4%)
  between operations  18 us (2%)
    psum x1, waiting for transfers between devices, local(): gram, cross = lax.psum((gram_part, cross_part), ('region', 'split'))  464 us
    all_to_all x2, blocking collectives, apply_blocks(): h_now = all_to_all(passed, 'split', 0, 0)  68 us
    another operation x7, other arithmetic, local(): lower = jnp.linalg.cholesky(gram)  42.1 us
    all_to_all x1, waiting for transfers between devices, apply_blocks(): h_now = all_to_all(passed, 'split', 0, 0)  29.1 us
    ppermute x6, waiting for transfers between devices, shifted(): return lax.ppermute(value, axis, pairs)  28.8 us
    ppermute x6, starting transfers between devices, shifted(): return lax.ppermute(value, axis, pairs)  28.6 us
    another operation x3, other arithmetic, local(): jax.scipy.linalg.solve_triangular(lower, filtered_two.T, lower=True)  22.8 us
  transfers between devices with their start and end apart: 8, of which 8 were waited for; matrix products, arithmetic and copies ran while one was open for 1% of the time, Pallas kernels for 0%

profile of v1, /device:TPU:1, one launch (start us, length us, event | category | flops | bytes accessed | tf_op | source)
XLA Modules:
  0.0 808.3 jit_solution(3798709986296327275)
XLA Ops:
  10.1 11.2 %all-to-all-start = ((bf16[8,3,192,256]{3,2,1,0:T(8,128)(2,1)}), bf16[8,3,192,256]{3,2,1,0:T(8,128)(2,1)}, u32[]{:S(2)}, u32[]{:S(2)}) async-start(bf16[8,3,192,256]{3,2,1,0:T(8,128)(2,1)} %stack.9), calls=%async_computation | async-start | bytes 4718592 | tf_op jit(solution)/shard_map/all_to_all | solution.py:20
  21.4 29.1 %all-to-all-done = bf16[8,3,192,256]{3,2,1,0:T(8,128)(2,1)} async-done(((bf16[8,3,192,256]{3,2,1,0:T(8,128)(2,1)}), bf16[8,3,192,256]{3,2,1,0:T(8,128)(2,1)}, u32[]{:S(2)}, u32[]{:S(2)}) %all-to-all-start) | async-done | bytes 2359328 | tf_op jit(solution)/shard_map/all_to_all | solution.py:20
  58.6 8.1 %collective-permute-start.1 = (bf16[6,192,256]{2,1,0:T(8,128)(2,1)}, bf16[6,192,256]{2,1,0:T(8,128)(2,1)}, u32[]{:S(2)}, u32[]{:S(2)}) collective-permute-start(bf16[6,192,256]{2,1,0:T(8,128)(2,1)} %gather_fusion.1), channel_id=1, source_target_pairs={{0,504},{8,0},{16,8},{24,16},{32,24},{40,32},{48,40},{56,48},{64,5... | collective-permute-start | bytes 1769480 | tf_op jit(solution)/shard_map/ppermute | solution.py:11
  70.6 4.2 collective-permute-done
  74.8 4.0 collective-permute-done.1
  78.8 3.5 pad_maximum_fusion
  82.2 4.8 gather_fusion.2
  90.5 34.0 %all_to_all.15 = bf16[8,3,192,256]{3,2,1,0:T(8,128)(2,1)} all-to-all(bf16[8,3,192,256]{3,2,1,0:T(8,128)(2,1)S(1)} %stack.10), channel_id=1, replica_groups=mesh['region'=64,'split'=8] {'split'}, dimensions={0} | all-to-all | bytes 4718592 | tf_op jit(solution)/shard_map/all_to_all | solution.py:20
  132.6 7.4 collective-permute-start.3
  140.0 10.9 %collective-permute-done.2 = bf16[6,192,256]{2,1,0:T(8,128)(2,1)S(1)} collective-permute-done((bf16[6,192,256]{2,1,0:T(8,128)(2,1)}, bf16[6,192,256]{2,1,0:T(8,128)(2,1)S(1)}, u32[]{:S(2)}, u32[]{:S(2)}) %collective-permute-start.2) | collective-permute-done | bytes 589856 | tf_op jit(solution)/shard_map/ppermute | solution.py:11
  151.9 3.3 pad_maximum_fusion.1
  155.2 4.8 gather_fusion.5
  164.4 34.1 %all_to_all.16 = bf16[8,3,192,256]{3,2,1,0:T(8,128)(2,1)} all-to-all(bf16[8,3,192,256]{3,2,1,0:T(8,128)(2,1)S(1)} %stack.11), channel_id=1, replica_groups=mesh['region'=64,'split'=8] {'split'}, dimensions={0} | all-to-all | bytes 4718592 | tf_op jit(solution)/shard_map/all_to_all | solution.py:20
  206.6 7.3 collective-permute-start.5
  213.9 3.3 fusion.42
  217.2 7.7 collective-permute-done.4
  225.8 3.3 pad_maximum_fusion.2
  229.1 4.8 gather_fusion.8
  239.0 463.5 %all-reduce.4.cloned.1.call-done = (f32[256,256]{0,1:T(8,128)}, f32[256,256]{0,1:T(8,128)}) async-done(((f32[256,256]{0,1:T(8,128)}, f32[256,256]{0,1:T(8,128)}), (f32[256,256]{0,1:T(8,128)}, f32[256,256]{0,1:T(8,128)})) %all-reduce.4.cloned.1.call-update) | async-done | bytes 524304 | tf_op jit(solution)/shard_map/psum | solution.py:52
  708.5 13.2 %cholesky.50 = f32[128,128]{1,0:T(8,128)} custom-call(f32[128,128]{1,0:T(8,128)} %cholesky.118), custom_call_target="Cholesky" | custom-call | tf_op jit(solution)/shard_map/jit(cholesky)/cholesky | solution.py:55
  724.7 11.3 %custom-call.18 = f32[1,128,128]{1,2,0:T(8,128)} custom-call(f32[1,128,128]{2,1,0:T(8,128)} %get-tuple-element.46), custom_call_target="InvertDiagBlocksLowerTriangular" | custom-call | tf_op jit(solution)/shard_map/jit(cholesky)/cholesky | solution.py:55
  739.4 13.4 %cholesky.105 = f32[128,128]{1,0:T(8,128)} custom-call(f32[128,128]{1,0:T(8,128)} %convolution_subtract_fusion.3), custom_call_target="Cholesky" | custom-call | tf_op jit(solution)/shard_map/jit(cholesky)/cholesky | solution.py:55
  758.6 7.0 while.5
  765.6 21.1 %custom-call.19 = f32[2,128,128]{1,2,0:T(8,128)} custom-call(f32[2,128,128]{2,1,0:T(8,128)} %get-tuple-element.18), custom_call_target="InvertDiagBlocksLowerTriangular" | custom-call | tf_op jit(solution)/shard_map/jit(_solve_triangular)/triangular_solve | solution.py:56
  (85 shorter events, 82.0 us)
Async XLA Ops:
  7.2 79.9 %copy-start = (bf16[3,12,192,192]{3,2,1,0:T(8,128)(2,1)S(1)}, bf16[3,12,192,192]{3,2,1,0:T(8,128)(2,1)}, u32[]{:S(2)}) copy-start(bf16[3,12,192,192]{3,2,1,0:T(8,128)(2,1)} %param.9) | copy-start | bytes 7962628
  8.4 12.9 %copy-start.9 = (s32[1,2,6]{2,1,0:T(2,128)S(1)}, s32[1,2,6]{2,1,0:T(2,128)}, u32[]{:S(2)}) copy-start(s32[1,2,6]{2,1,0:T(2,128)} %param.12) | copy-start | bytes 148
  10.1 56.6 %copy-start.8 = (f32[2]{0:T(128)S(1)}, f32[2]{0:T(128)}, u32[]{:S(2)}) copy-start(f32[2]{0:T(128)} %param.13) | copy-start | bytes 28
  10.1 59.6 %copy-start.7 = (s32[3,12]{1,0:T(4,128)S(1)}, s32[3,12]{1,0:T(4,128)}, u32[]{:S(2)}) copy-start(s32[3,12]{1,0:T(4,128)} %param.10) | copy-start | bytes 436
  10.1 40.4 %all-to-all-start = ((bf16[8,3,192,256]{3,2,1,0:T(8,128)(2,1)}), bf16[8,3,192,256]{3,2,1,0:T(8,128)(2,1)}, u32[]{:S(2)}, u32[]{:S(2)}) async-start(bf16[8,3,192,256]{3,2,1,0:T(8,128)(2,1)} %stack.9), calls=%async_computation | async-start | bytes 4718592 | tf_op jit(solution)/shard_map/all_to_all | solution.py:20
  21.4 681.1 %all-reduce.4.cloned.1.call-start = ((), (), s32[]{:S(2)}) async-start(), calls=%async_computation.3 | async-start | bytes 1048576 | tf_op jit(solution)/shard_map/psum | solution.py:52
  53.6 21.2 %collective-permute-start = (bf16[6,192,256]{2,1,0:T(8,128)(2,1)}, bf16[6,192,256]{2,1,0:T(8,128)(2,1)}, u32[]{:S(2)}, u32[]{:S(2)}) collective-permute-start(bf16[6,192,256]{2,1,0:T(8,128)(2,1)} %gather_fusion), channel_id=1, source_target_pairs={{0,8},{8,16},{16,24},{24,32},{32,40},{40,48},{48,56},{56,64},{64,7... | collective-permute-start | bytes 1769480 | tf_op jit(solution)/shard_map/ppermute | solution.py:11
  58.6 20.2 %collective-permute-start.1 = (bf16[6,192,256]{2,1,0:T(8,128)(2,1)}, bf16[6,192,256]{2,1,0:T(8,128)(2,1)}, u32[]{:S(2)}, u32[]{:S(2)}) collective-permute-start(bf16[6,192,256]{2,1,0:T(8,128)(2,1)} %gather_fusion.1), channel_id=1, source_target_pairs={{0,504},{8,0},{16,8},{24,16},{32,24},{40,32},{48,40},{56,48},{64,5... | collective-permute-start | bytes 1769480 | tf_op jit(solution)/shard_map/ppermute | solution.py:11
  87.1 3.1 copy-start.2
  90.1 34.4 %copy-start.4 = (f32[3,256,192,1]{1,2,3,0:T(8,128)}, f32[3,256,192,1]{1,2,3,0:T(8,128)S(1)}, u32[]{:S(2)}) copy-start(f32[3,256,192,1]{1,2,3,0:T(8,128)S(1)} %fusion.4) | copy-start | bytes 1769476
  130.6 20.3 %collective-permute-start.2 = (bf16[6,192,256]{2,1,0:T(8,128)(2,1)}, bf16[6,192,256]{2,1,0:T(8,128)(2,1)S(1)}, u32[]{:S(2)}, u32[]{:S(2)}) collective-permute-start(bf16[6,192,256]{2,1,0:T(8,128)(2,1)} %gather_fusion.3), channel_id=1, source_target_pairs={{0,8},{8,16},{16,24},{24,32},{32,40},{40,48},{48,56},{56,64},{64,7... | collective-permute-start | bytes 1769480 | tf_op jit(solution)/shard_map/ppermute | solution.py:11
  132.6 19.4 %collective-permute-start.3 = (bf16[6,192,256]{2,1,0:T(8,128)(2,1)}, bf16[6,192,256]{2,1,0:T(8,128)(2,1)S(1)}, u32[]{:S(2)}, u32[]{:S(2)}) collective-permute-start(bf16[6,192,256]{2,1,0:T(8,128)(2,1)} %gather_fusion.4), channel_id=1, source_target_pairs={{0,504},{8,0},{16,8},{24,16},{32,24},{40,32},{48,40},{56,48},{64,5... | collective-permute-start | bytes 1769480 | tf_op jit(solution)/shard_map/ppermute | solution.py:11
  160.0 3.1 copy-start.3
  160.0 3.1 copy-start.5
  204.6 20.2 %collective-permute-start.4 = (bf16[6,192,256]{2,1,0:T(8,128)(2,1)}, bf16[6,192,256]{2,1,0:T(8,128)(2,1)S(1)}, u32[]{:S(2)}, u32[]{:S(2)}) collective-permute-start(bf16[6,192,256]{2,1,0:T(8,128)(2,1)} %gather_fusion.6), channel_id=1, source_target_pairs={{0,8},{8,16},{16,24},{24,32},{32,40},{40,48},{48,56},{56,64},{64,7... | collective-permute-start | bytes 1769480 | tf_op jit(solution)/shard_map/ppermute | solution.py:11
  206.6 19.3 %collective-permute-start.5 = (bf16[6,192,256]{2,1,0:T(8,128)(2,1)}, bf16[6,192,256]{2,1,0:T(8,128)(2,1)S(1)}, u32[]{:S(2)}, u32[]{:S(2)}) collective-permute-start(bf16[6,192,256]{2,1,0:T(8,128)(2,1)} %gather_fusion.7), channel_id=1, source_target_pairs={{0,504},{8,0},{16,8},{24,16},{32,24},{40,32},{48,40},{56,48},{64,5... | collective-permute-start | bytes 1769480 | tf_op jit(solution)/shard_map/ppermute | solution.py:11
  233.9 3.0 copy-start.1
  707.2 0.7 copy-start.6
Sparse Core Ops, SparseCore 0:
  239.1 463.3 all-reduce.3
